TPU v7x, 32 devices: a whole 2x2x4 slice. The times are simulated.
32 devices in a mesh: dp: 16 (over z, y, core), mp: 2 (over x).
Axes of the slice: x: 2, y: 2, z: 4, core: 2. Of those that a mesh axis runs over, the one named last changes fastest.
Arguments:
- tokens_in: bfloat16 [4096, 2048], P(('dp', 'mp')), may hold values from -6 to 6
- teacher: bfloat16 [4096, 2048], P(('dp', 'mp')), may hold values from -6 to 6
- valid_mask: int32 [16, 256], P('dp', 'mp'), may hold values from 0 to 1, as said below
- group_of: int32 [16], replicated, may hold values from 0 to 1, as said below
- prompt_len: int32 [2], replicated, may hold values from 128 to 256
- ln1_gain: bfloat16 [2048], P('dp'), may hold values from 0.5 to 1.5
- ln1_bias: bfloat16 [2048], P('dp'), may hold values from -2 to 2
- w_query: bfloat16 [2048, 2048], P('dp', 'mp'), may hold values from -0.125 to 0.125
- w_key: bfloat16 [2048, 2048], P('dp', 'mp'), may hold values from -0.125 to 0.125
- w_value: bfloat16 [2048, 4096], P('dp', 'mp'), may hold values from -0.125 to 0.125
- w_gate: bfloat16 [2048, 4096], P('dp', 'mp'), may hold values from -0.125 to 0.125
- w_out: bfloat16 [2048, 4096], P('dp', 'mp'), may hold values from -0.1875 to 0.1875
- ln2_gain: bfloat16 [2048], P('dp'), may hold values from 0.5 to 1.5
- ln2_bias: bfloat16 [2048], P('dp'), may hold values from -2 to 2
- w_up: bfloat16 [2048, 4096], P('dp', 'mp'), may hold values from -0.125 to 0.125
- w_down: bfloat16 [2048, 4096], P('dp', 'mp'), may hold values from -0.125 to 0.125
Outputs:
- block_out: float32 [4096, 2048], P(('dp', 'mp'))
- grad_tokens: float32 [4096, 2048], P(('dp', 'mp'))
- loss: float32 [], replicated
- grad_ln1_gain: float32 [2048], P('dp')
- grad_ln1_bias: float32 [2048], P('dp')
- grad_w_query: float32 [2048, 2048], P('dp', 'mp')
- grad_w_key: float32 [2048, 2048], P('dp', 'mp')
- grad_w_value: float32 [2048, 4096], P('dp', 'mp')
- grad_w_gate: float32 [2048, 4096], P('dp', 'mp')
- grad_w_out: float32 [2048, 4096], P('dp', 'mp')
- grad_ln2_gain: float32 [2048], P('dp')
- grad_ln2_bias: float32 [2048], P('dp')
- grad_w_up: float32 [2048, 4096], P('dp', 'mp')
- grad_w_down: float32 [2048, 4096], P('dp', 'mp')
Inputs may be any that keep to these rules, and one draw needn't show every extreme that they name: `valid_mask`: in each row the ones form a leading run of one or more positions, zeros follow. `group_of`: each group number is held by exactly 8 segments; a group's prompt is its lowest-numbered segment, the others are its continuations.
All inputs are finite; a program needn't handle non-finite values.
Results may differ from a plain program's by a relative error of at most 0.013.
Values may be sent and summed in bfloat16 or wider, within the bound.
A program may use at most 192 MiB of HBM per device.

v0:
```python
import math
import jax
import jax.numpy as jnp
from jax import lax
from jax.sharding import PartitionSpec as P

DK = 256
DV = 512
EPSILON = 1e-05
GROUP_EPSILON = 0.05


def norm_stats(values, floor_eps):
    center = jnp.mean(values, axis=-1, keepdims=True)
    shifted = values - center
    inv_std = lax.rsqrt(jnp.mean(shifted * shifted, axis=-1, keepdims=True) + floor_eps)
    return (shifted * inv_std, inv_std)


def norm_back(grad_in, normed, inv_std):
    mean_grad = jnp.mean(grad_in, axis=-1, keepdims=True)
    mean_proj = jnp.mean(grad_in * normed, axis=-1, keepdims=True)
    return (grad_in - mean_grad - normed * mean_proj) * inv_std


def xpos_tables(positions, direction):
    half_dim = DK // 2
    pair_index = jnp.arange(half_dim, dtype=jnp.float32)
    frequency = jnp.exp(-(2.0 * pair_index / DK) * math.log(10000.0))
    base_ratio = (2.0 * pair_index / DK + 0.4) / 1.4
    angles = positions[:, None] * frequency[None, :]
    factor = jnp.exp(direction * (positions[:, None] / 512.0) * jnp.log(base_ratio)[None, :])
    return (jnp.cos(angles), jnp.sin(angles), factor)


def rotate_pairs(values, cosine, sine_tab, factor):
    half_dim = values.shape[-1] // 2
    first_half = values[..., :half_dim]
    second = values[..., half_dim:]
    cosine = cosine[:, None, :]
    sine_tab = sine_tab[:, None, :]
    factor = factor[:, None, :]
    return jnp.concatenate(
        [
            (first_half * cosine - second * sine_tab) * factor,
            (second * cosine + first_half * sine_tab) * factor,
        ],
        axis=-1,
    )


def rotate_back(grad_rot, cosine, sine_tab, factor):
    half_dim = grad_rot.shape[-1] // 2
    first_half = grad_rot[..., :half_dim]
    second = grad_rot[..., half_dim:]
    cosine = cosine[:, None, :]
    sine_tab = sine_tab[:, None, :]
    factor = factor[:, None, :]
    return jnp.concatenate(
        [
            (first_half * cosine + second * sine_tab) * factor,
            (second * cosine - first_half * sine_tab) * factor,
        ],
        axis=-1,
    )


def plain_dot(first_op, second_op):
    return jnp.dot(first_op, second_op, preferred_element_type=jnp.float32)


def contract_last(first_op, second_op):
    return lax.dot_general(
        first_op, second_op, (((1,), (1,)), ((), ())), preferred_element_type=jnp.float32
    )


def contract_first(first_op, second_op):
    return lax.dot_general(
        first_op, second_op, (((0,), (0,)), ((), ())), preferred_element_type=jnp.float32
    )


def gather_rows(rows_low):
    return lax.all_gather(rows_low, "mp", axis=0, tiled=True)


def scatter_rows(terms):
    return lax.psum_scatter(terms, "mp", scatter_dimension=0, tiled=True)


def on_device(
    tokens_in,
    teacher,
    valid_mask,
    group_of,
    prompt_len,
    ln1_gain,
    ln1_bias,
    w_query,
    w_key,
    w_value,
    w_gate,
    w_out,
    ln2_gain,
    ln2_bias,
    w_up,
    w_down,
):
    half_rows = tokens_in.shape[0]
    model_dim = tokens_in.shape[1]
    seg_len = half_rows * lax.axis_size("mp")
    seg_count = group_of.shape[0]
    group_count = prompt_len.shape[0]
    heads_local = w_query.shape[1] // DK
    token_total = seg_len * seg_count
    dp_index = lax.axis_index("dp")
    mp_index = lax.axis_index("mp")
    attn_full = (
        lax.all_gather(ln1_gain, "dp", axis=0, tiled=True),
        lax.all_gather(ln1_bias, "dp", axis=0, tiled=True),
        lax.all_gather(w_query, "dp", axis=0, tiled=True),
        lax.all_gather(w_key, "dp", axis=0, tiled=True),
        lax.all_gather(w_value, "dp", axis=0, tiled=True),
        lax.all_gather(w_gate, "dp", axis=0, tiled=True),
        lax.all_gather(w_out, "dp", axis=0, tiled=True),
    )
    ffn_full = (
        lax.all_gather(ln2_gain, "dp", axis=0, tiled=True),
        lax.all_gather(ln2_bias, "dp", axis=0, tiled=True),
        lax.all_gather(w_up, "dp", axis=0, tiled=True),
        lax.all_gather(w_down, "dp", axis=0, tiled=True),
    )
    gain_one = attn_full[0].astype(jnp.float32)
    bias_one = attn_full[1].astype(jnp.float32)
    wq_full, wk_full, wv_full, wg_full, wo_full = (
        attn_full[2],
        attn_full[3],
        attn_full[4],
        attn_full[5],
        attn_full[6],
    )
    gain_two = ffn_full[0].astype(jnp.float32)
    bias_two = ffn_full[1].astype(jnp.float32)
    wu_full, wd_full = (ffn_full[2], ffn_full[3])
    segment_ids = jnp.arange(seg_count, dtype=jnp.int32)
    my_group = jnp.sum(jnp.where(segment_ids == dp_index, group_of, 0))
    first_member = jnp.min(jnp.where(group_of == my_group, segment_ids, seg_count))
    prompt_flag = (first_member == dp_index).astype(jnp.float32)
    group_match = jnp.arange(group_count, dtype=jnp.int32) == my_group
    group_onehot = group_match.astype(jnp.float32)
    prompt_size = jnp.sum(jnp.where(group_match, prompt_len, 0))
    token_ids = jnp.arange(seg_len, dtype=jnp.int32)
    offset = jnp.where(prompt_flag > 0, 0, prompt_size)
    positions = (token_ids + offset).astype(jnp.float32)
    head_ids = (mp_index * heads_local + jnp.arange(heads_local, dtype=jnp.int32)).astype(
        jnp.float32
    )
    log_decay = jnp.log(1.0 - 2.0 ** (-5.0 - head_ids))
    before_end = token_ids < prompt_size
    state_age = (prompt_size - 1 - token_ids).astype(jnp.float32)
    state_weighting = jnp.where(
        (before_end & (prompt_flag > 0))[:, None],
        jnp.exp(log_decay[None, :] * jnp.maximum(state_age, 0.0)[:, None]),
        0.0,
    )
    continuation_factor = (1.0 - prompt_flag) * jnp.exp(
        log_decay[None, :] * (token_ids.astype(jnp.float32) + 1.0)[:, None]
    )
    float_ids = token_ids.astype(jnp.float32)
    distance = float_ids[:, None] - float_ids[None, :]
    decay_mat = jnp.where(
        distance[None] >= 0.0,
        jnp.exp(log_decay[:, None, None] * jnp.maximum(distance, 0.0)[None]),
        0.0,
    )
    own_ids = mp_index * half_rows + jnp.arange(half_rows, dtype=jnp.int32)
    loss_mask = valid_mask[0].astype(jnp.float32) * jnp.where(
        prompt_flag > 0, own_ids < prompt_size, True
    ).astype(jnp.float32)
    token_rows = tokens_in.astype(jnp.float32)
    normed_one, inv_one = norm_stats(token_rows, EPSILON)
    a_all = gather_rows((normed_one * gain_one + bias_one).astype(jnp.bfloat16))
    queries = plain_dot(a_all, wq_full).reshape(seg_len, heads_local, DK)
    keys_raw = plain_dot(a_all, wk_full).reshape(seg_len, heads_local, DK)
    reduced_values = (
        plain_dot(a_all, wv_full).astype(jnp.bfloat16).reshape(seg_len, heads_local, DV)
    )
    gate_pre = plain_dot(a_all, wg_full)
    cosine, sine_tab, grow_fac = xpos_tables(positions, 1.0)
    _, _, shrink = xpos_tables(positions, -1.0)
    q_scale = DK ** (-0.5)
    rotated_queries = (rotate_pairs(queries, cosine, sine_tab, grow_fac) * q_scale).astype(
        jnp.bfloat16
    )
    rotated_keys = rotate_pairs(keys_raw, cosine, sine_tab, shrink).astype(jnp.bfloat16)
    local_state = jnp.einsum(
        "jld,jla->lda",
        rotated_keys.astype(jnp.float32) * state_weighting[:, :, None],
        reduced_values.astype(jnp.float32),
        precision=lax.Precision.HIGHEST,
    )
    slots = group_onehot[:, None, None, None] * (prompt_flag * local_state)[None]
    summed = lax.psum(slots, "dp")
    state_lookup = jnp.sum(summed * group_onehot[:, None, None, None], axis=0).astype(jnp.bfloat16)
    scores = jnp.einsum(
        "thk,nhk->htn", rotated_queries, rotated_keys, preferred_element_type=jnp.float32
    )
    weights_low = (scores * decay_mat).astype(jnp.bfloat16)
    retained_output = jnp.einsum(
        "htn,nhv->thv", weights_low, reduced_values, preferred_element_type=jnp.float32
    )
    carried_forward = jnp.einsum(
        "ozi,ziw->ozw", rotated_queries, state_lookup, preferred_element_type=jnp.float32
    )
    retained_output = retained_output + continuation_factor[:, :, None] * carried_forward
    grouped, inv_group = norm_stats(retained_output, GROUP_EPSILON)
    gate_act = jax.nn.silu(gate_pre).reshape(seg_len, heads_local, DV)
    gated_out = (gate_act * grouped).reshape(seg_len, heads_local * DV).astype(jnp.bfloat16)
    attn_own = scatter_rows(contract_last(gated_out, wo_full))
    hidden_res = token_rows + attn_own
    normed_two, inv_two = norm_stats(hidden_res, EPSILON)
    c_all = gather_rows((normed_two * gain_two + bias_two).astype(jnp.bfloat16))
    up_pre = plain_dot(c_all, wu_full)
    up_act = jax.nn.gelu(up_pre, approximate=False).astype(jnp.bfloat16)
    ffn_own = scatter_rows(contract_last(up_act, wd_full))
    block_out = hidden_res + ffn_own
    error_rows = block_out - teacher.astype(jnp.float32)
    weighted = loss_mask[:, None] * error_rows
    valid_count, squared = lax.psum(
        (jnp.sum(loss_mask), jnp.sum(weighted * error_rows)), ("dp", "mp")
    )
    grad_out = token_total / valid_count * weighted
    loss_value = squared / (valid_count * model_dim)
    grad_ffn_all = gather_rows(grad_out.astype(jnp.bfloat16))
    grad_up_act = plain_dot(grad_ffn_all, wd_full)
    _, gelu_pull = jax.vjp(lambda inner: jax.nn.gelu(inner, approximate=False), up_pre)
    grad_up = gelu_pull(grad_up_act)[0].astype(jnp.bfloat16)
    grad_wd = contract_first(grad_ffn_all, up_act)
    grad_wu = contract_first(c_all, grad_up)
    grad_c = scatter_rows(contract_last(grad_up, wu_full))
    grad_gain2_part = jnp.sum(grad_c * normed_two, axis=0)
    grad_bias2_part = jnp.sum(grad_c, axis=0)
    grad_hidden = grad_out + norm_back(grad_c * gain_two, normed_two, inv_two)
    ffn_reduced = (
        lax.psum_scatter(grad_gain2_part, "dp", scatter_dimension=0, tiled=True),
        lax.psum_scatter(grad_bias2_part, "dp", scatter_dimension=0, tiled=True),
        lax.psum_scatter(grad_wu, "dp", scatter_dimension=0, tiled=True),
        lax.psum_scatter(grad_wd, "dp", scatter_dimension=0, tiled=True),
    )
    grad_attn_all = gather_rows(grad_hidden.astype(jnp.bfloat16))
    grad_gated = plain_dot(grad_attn_all, wo_full).reshape(seg_len, heads_local, DV)
    grad_wo = contract_first(grad_attn_all, gated_out)
    _, silu_pull = jax.vjp(jax.nn.silu, gate_pre)
    grad_gate = silu_pull((grad_gated * grouped).reshape(seg_len, heads_local * DV))[0].astype(
        jnp.bfloat16
    )
    retained_gradient = norm_back(grad_gated * gate_act, grouped, inv_group).astype(jnp.bfloat16)
    grad_weights = jnp.einsum(
        "thv,nhv->htn", retained_gradient, reduced_values, preferred_element_type=jnp.float32
    )
    grad_values = jnp.einsum(
        "htn,thv->nhv", weights_low, retained_gradient, preferred_element_type=jnp.float32
    )
    grad_scores = (grad_weights * decay_mat).astype(jnp.bfloat16)
    grad_q_rot = jnp.einsum(
        "htn,nhk->thk", grad_scores, rotated_keys, preferred_element_type=jnp.float32
    )
    grad_q_rot = grad_q_rot + continuation_factor[:, :, None] * jnp.einsum(
        "mjr,jwr->mjw", retained_gradient, state_lookup, preferred_element_type=jnp.float32
    )
    grad_k_rot = jnp.einsum(
        "htn,thk->nhk", grad_scores, rotated_queries, preferred_element_type=jnp.float32
    )
    state_grad_own = jnp.einsum(
        "ybn,ybw->bnw",
        rotated_queries.astype(jnp.float32) * continuation_factor[:, :, None],
        retained_gradient.astype(jnp.float32),
        precision=lax.Precision.HIGHEST,
    )
    grad_slots = group_onehot[:, None, None, None] * state_grad_own[None]
    grad_summed = lax.psum(grad_slots, "dp")
    state_gradient = (
        prompt_flag * jnp.sum(grad_summed * group_onehot[:, None, None, None], axis=0)
    ).astype(jnp.bfloat16)
    grad_k_rot = grad_k_rot + state_weighting[:, :, None] * jnp.einsum(
        "ilm,lpm->ilp", reduced_values, state_gradient, preferred_element_type=jnp.float32
    )
    grad_values = grad_values + state_weighting[:, :, None] * jnp.einsum(
        "zdo,doi->zdi", rotated_keys, state_gradient, preferred_element_type=jnp.float32
    )
    grad_queries = (
        rotate_back(grad_q_rot * q_scale, cosine, sine_tab, grow_fac)
        .reshape(seg_len, heads_local * DK)
        .astype(jnp.bfloat16)
    )
    grad_keys = (
        rotate_back(grad_k_rot, cosine, sine_tab, shrink)
        .reshape(seg_len, heads_local * DK)
        .astype(jnp.bfloat16)
    )
    grad_vlow = grad_values.reshape(seg_len, heads_local * DV).astype(jnp.bfloat16)
    grad_wq = contract_first(a_all, grad_queries)
    grad_wk = contract_first(a_all, grad_keys)
    grad_wv = contract_first(a_all, grad_vlow)
    grad_wg = contract_first(a_all, grad_gate)
    grad_a_terms = (
        contract_last(grad_queries, wq_full)
        + contract_last(grad_keys, wk_full)
        + contract_last(grad_vlow, wv_full)
        + contract_last(grad_gate, wg_full)
    )
    grad_a = scatter_rows(grad_a_terms)
    grad_gain1_part = jnp.sum(grad_a * normed_one, axis=0)
    grad_bias1_part = jnp.sum(grad_a, axis=0)
    grad_tokens = grad_hidden + norm_back(grad_a * gain_one, normed_one, inv_one)
    attn_reduced = (
        lax.psum_scatter(grad_gain1_part, "dp", scatter_dimension=0, tiled=True),
        lax.psum_scatter(grad_bias1_part, "dp", scatter_dimension=0, tiled=True),
        lax.psum_scatter(grad_wq, "dp", scatter_dimension=0, tiled=True),
        lax.psum_scatter(grad_wk, "dp", scatter_dimension=0, tiled=True),
        lax.psum_scatter(grad_wv, "dp", scatter_dimension=0, tiled=True),
        lax.psum_scatter(grad_wg, "dp", scatter_dimension=0, tiled=True),
        lax.psum_scatter(grad_wo, "dp", scatter_dimension=0, tiled=True),
    )
    norm_sums = lax.psum((attn_reduced[0], attn_reduced[1], ffn_reduced[0], ffn_reduced[1]), "mp")
    return (
        block_out,
        grad_tokens,
        loss_value,
        norm_sums[0],
        norm_sums[1],
        attn_reduced[2],
        attn_reduced[3],
        attn_reduced[4],
        attn_reduced[5],
        attn_reduced[6],
        norm_sums[2],
        norm_sums[3],
        ffn_reduced[2],
        ffn_reduced[3],
    )


def solution(mesh):
    return jax.shard_map(
        on_device,
        mesh=mesh,
        in_specs=(
            P(("dp", "mp"), None),
            P(("dp", "mp"), None),
            P("dp", "mp"),
            P(),
            P(),
            P("dp"),
            P("dp"),
            P("dp", "mp"),
            P("dp", "mp"),
            P("dp", "mp"),
            P("dp", "mp"),
            P("dp", "mp"),
            P("dp"),
            P("dp"),
            P("dp", "mp"),
            P("dp", "mp"),
        ),
        out_specs=(
            P(("dp", "mp"), None),
            P(("dp", "mp"), None),
            P(),
            P("dp"),
            P("dp"),
            P("dp", "mp"),
            P("dp", "mp"),
            P("dp", "mp"),
            P("dp", "mp"),
            P("dp", "mp"),
            P("dp"),
            P("dp"),
            P("dp", "mp"),
            P("dp", "mp"),
        ),
        check_vma=False,
    )
```

profile of v0, /device:TPU:0, one launch (start us, length us, event | category | flops | bytes accessed | tf_op | source)
XLA Modules:
  0.0 2218.7 jit_solution(17705684298100000474)
XLA Ops:
  9.8 23.3 %all-gather = bf16[16,1,128]{2,1,0:T(2,128)(2,1)S(1)} all-gather(bf16[1,1,128]{2,1,0:T(2,128)(2,1)} %bitcast.140), channel_id=1, replica_groups=mesh['dp'=16,'mp'=2] {'dp'}, dimensions={0}, use_global_device_ids=true | all-gather | bytes 4352 | tf_op jit(solution)/shard_map/all_gather | solution.py:120
  33.1 17.6 all-gather.1
  50.8 2.2 fusion.28
  64.5 8.4 all-gather.16.cloned.1.call-done
  72.8 52.6 %all-gather.24.cloned.1.call-done = bf16[2048,1024]{1,0:T(8,128)(2,1)} async-done(((bf16[128,1024]{1,0:T(8,128)(2,1)}), bf16[2048,1024]{1,0:T(8,128)(2,1)}) %all-gather.24.cloned.1.call-update) | async-done | bytes 4194320 | tf_op jit(solution)/shard_map/all_gather | solution.py:123
  125.4 3.8 fusion.70
  129.7 46.8 %all-gather.22.cloned.1.call-done = bf16[2048,1024]{1,0:T(8,128)(2,1)} async-done(((bf16[128,1024]{1,0:T(8,128)(2,1)}), bf16[2048,1024]{1,0:T(8,128)(2,1)}) %all-gather.22.cloned.1.call-update) | async-done | bytes 4194320 | tf_op jit(solution)/shard_map/all_gather | solution.py:122
  176.5 4.4 fusion.69
  185.0 66.4 %all-gather.20.cloned.1.call-done = bf16[2048,2048]{1,0:T(8,128)(2,1)} async-done(((bf16[128,2048]{1,0:T(8,128)(2,1)}), bf16[2048,2048]{1,0:T(8,128)(2,1)}) %all-gather.20.cloned.1.call-update) | async-done | bytes 8388624 | tf_op jit(solution)/shard_map/all_gather | solution.py:124
  251.4 5.7 convolution_convert_fusion
  258.5 2.6 broadcast_multiply_fusion.1
  265.3 61.1 %all-gather.18.cloned.1.call-done = bf16[2048,2048]{1,0:T(8,128)(2,1)} async-done(((bf16[128,2048]{1,0:T(8,128)(2,1)}), bf16[2048,2048]{1,0:T(8,128)(2,1)}) %all-gather.18.cloned.1.call-update) | async-done | bytes 8388624 | tf_op jit(solution)/shard_map/all_gather | solution.py:125
  326.3 7.8 fusion.12
  334.1 3.0 copy.151
  337.1 1.9 fusion.36
  339.0 100.7 %all-reduce.10.cloned.1.call-done = f32[2,4,256,512]{3,2,1,0:T(8,128)} async-done(((f32[2,4,256,512]{3,2,1,0:T(8,128)}), f32[2,4,256,512]{3,2,1,0:T(8,128)}) %all-reduce.10.cloned.1.call-update) | async-done | bytes 4194320 | tf_op jit(solution)/shard_map/psum | solution.py:204
  439.7 3.0 multiply_reduce_fusion.1
  445.8 69.5 %all-gather.26.cloned.1.call-done = bf16[2048,2048]{1,0:T(8,128)(2,1)} async-done(((bf16[128,2048]{1,0:T(8,128)(2,1)}), bf16[2048,2048]{1,0:T(8,128)(2,1)}) %all-gather.26.cloned.1.call-update) | async-done | bytes 8388624 | tf_op jit(solution)/shard_map/all_gather | solution.py:126
  515.3 7.1 fusion.71
  523.2 19.0 all-gather.2
  542.2 17.4 all-gather.3
  564.7 64.9 %all-gather.30.cloned.1.call-done = bf16[2048,2048]{1,0:T(8,128)(2,1)} async-done(((bf16[128,2048]{1,0:T(8,128)(2,1)}), bf16[2048,2048]{1,0:T(8,128)(2,1)}) %all-gather.30.cloned.1.call-update) | async-done | bytes 8388624 | tf_op jit(solution)/shard_map/all_gather | solution.py:131
  629.6 21.9 all-gather.28.cloned.1.call-done
  651.4 10.6 multiply_convert_fusion.2
  662.1 65.9 %all-gather.32.cloned.1.call-done = bf16[2048,2048]{1,0:T(8,128)(2,1)} async-done(((bf16[128,2048]{1,0:T(8,128)(2,1)}), bf16[2048,2048]{1,0:T(8,128)(2,1)}) %all-gather.32.cloned.1.call-update) | async-done | bytes 8388624 | tf_op jit(solution)/shard_map/all_gather | solution.py:132
  727.9 7.4 fusion.72
  735.4 2.4 fusion.63
  737.8 28.2 %reduce-scatter.14.cloned.1.call-done = f32[128,2048]{1,0:T(8,128)} async-done(((f32[256,2048]{1,0:T(8,128)}), f32[128,2048]{1,0:T(8,128)}) %reduce-scatter.14.cloned.1.call-update) | async-done | bytes 1048592 | tf_op jit(solution)/shard_map/reduce_scatter | solution.py:89
  766.0 3.2 fusion.35
  769.2 39.5 %all-reduce.4 = (f32[]{:T(128)}, f32[]{:T(128)}) all-reduce(f32[]{:T(128)} %get-tuple-element.39, f32[]{:T(128)} %get-tuple-element.37), channel_id=1, replica_groups=mesh['dp'=16,'mp'=2] {'dp','mp'}, use_global_device_ids=true, to_apply=%region_14.15 | all-reduce | flops 2 | bytes 16 | tf_op jit(solution)/shard_map/psum | solution.py:230
  809.5 2.3 fusion.47
  811.9 22.3 %all-gather.34.cloned.1.call-done = bf16[256,2048]{1,0:T(8,128)(2,1)} async-done(((bf16[128,2048]{1,0:T(8,128)(2,1)}), bf16[256,2048]{1,0:T(8,128)(2,1)}) %all-gather.34.cloned.1.call-update) | async-done | bytes 1048592 | tf_op jit(solution)/shard_map/all_gather | solution.py:85
  834.2 7.7 add_convert_fusion
  842.9 7.1 fusion.73
  850.2 31.8 %reduce-scatter.16.cloned.1.call-done = f32[128,2048]{1,0:T(8,128)} async-done(((f32[256,2048]{1,0:T(8,128)}), f32[128,2048]{1,0:T(8,128)}) %reduce-scatter.16.cloned.1.call-update) | async-done | bytes 1048592 | tf_op jit(solution)/shard_map/reduce_scatter | solution.py:89
  882.1 2.4 multiply_reduce_fusion.4
  884.5 3.1 fusion.62
  887.6 21.4 all-gather.36.cloned.1.call-done
  909.0 7.2 fusion.74
  919.1 2.0 fusion.42
  921.2 2.6 broadcast_multiply_fusion
  923.9 3.4 copy.150
  934.9 1.9 fusion.3
  936.8 98.4 %all-reduce.12.cloned.1.call-done = f32[2,4,256,512]{3,2,1,0:T(8,128)} async-done(((f32[2,4,256,512]{3,2,1,0:T(8,128)}), f32[2,4,256,512]{3,2,1,0:T(8,128)}) %all-reduce.12.cloned.1.call-update) | async-done | bytes 4194320 | tf_op jit(solution)/shard_map/psum | solution.py:282
  1035.1 3.1 multiply_reduce_fusion
  1042.0 3.6 fusion.75
  1047.0 6.0 convolution_add_fusion.2
  1053.0 3.9 convolution_add_fusion.1
  1058.1 4.8 fusion.78
  1063.0 4.6 fusion.77
  1068.9 9.4 fusion.82
  1079.5 9.4 fusion.83
  1090.0 9.8 fusion.81
  1100.2 9.8 fusion.80
  1111.3 8.1 fusion.79
  1124.5 62.8 %all-reduce.5 = (f32[2048]{0:T(1024)S(1)}, f32[2048]{0:T(1024)S(1)}, f32[2048]{0:T(1024)S(1)}, f32[2048]{0:T(1024)S(1)}) all-reduce(f32[2048]{0:T(1024)S(1)} %get-tuple-element.18, f32[2048]{0:T(1024)S(1)} %get-tuple-element.23, f32[2048]{0:T(1024)S(1)} %copy-done.51, ...), channel_id=6, replica_groups=mesh['dp'=16,'mp'=2] {'dp'}, use_global_device_ids=true, to_apply=%region_28.29.clone | all-reduce | flops 8192 | bytes 65536
  1187.6 5.4 all-reduce.6
  1194.5 2.3 reduce-scatter.22.cloned.1.call-done
  1196.8 107.8 %reduce-scatter.20.cloned.1.call-done = f32[128,1024]{1,0:T(8,128)} async-done(((f32[2048,1024]{1,0:T(8,128)}), f32[128,1024]{1,0:T(8,128)}) %reduce-scatter.20.cloned.1.call-update) | async-done | bytes 524304 | tf_op jit(solution)/shard_map/reduce_scatter | solution.py:320
  1304.6 181.5 %reduce-scatter.30.cloned.1.call-done = f32[128,2048]{1,0:T(8,128)} async-done(((f32[2048,2048]{1,0:T(8,128)}), f32[128,2048]{1,0:T(8,128)}) %reduce-scatter.30.cloned.1.call-update) | async-done | bytes 1048592 | tf_op jit(solution)/shard_map/reduce_scatter | solution.py:248
  1486.1 181.1 %reduce-scatter.32.cloned.1.call-done = f32[128,2048]{1,0:T(8,128)} async-done(((f32[2048,2048]{1,0:T(8,128)}), f32[128,2048]{1,0:T(8,128)}) %reduce-scatter.32.cloned.1.call-update) | async-done | bytes 1048592 | tf_op jit(solution)/shard_map/reduce_scatter | solution.py:249
  1667.3 181.1 %reduce-scatter.28.cloned.1.call-done = f32[128,2048]{1,0:T(8,128)} async-done(((f32[2048,2048]{1,0:T(8,128)}), f32[128,2048]{1,0:T(8,128)}) %reduce-scatter.28.cloned.1.call-update) | async-done | bytes 1048592 | tf_op jit(solution)/shard_map/reduce_scatter | solution.py:324
  1848.4 181.1 %reduce-scatter.26.cloned.1.call-done = f32[128,2048]{1,0:T(8,128)} async-done(((f32[2048,2048]{1,0:T(8,128)}), f32[128,2048]{1,0:T(8,128)}) %reduce-scatter.26.cloned.1.call-update) | async-done | bytes 1048592 | tf_op jit(solution)/shard_map/reduce_scatter | solution.py:323
  2029.5 181.0 %reduce-scatter.24.cloned.1.call-done = f32[128,2048]{1,0:T(8,128)} async-done(((f32[2048,2048]{1,0:T(8,128)}), f32[128,2048]{1,0:T(8,128)}) %reduce-scatter.24.cloned.1.call-update) | async-done | bytes 1048592 | tf_op jit(solution)/shard_map/reduce_scatter | solution.py:322
  (267 shorter events, 58.7 us)
Async XLA Ops:
  7.2 48.6 %copy-start.68 = (s32[16]{0:T(128)S(1)}, s32[16]{0:T(128)}, u32[]{:S(2)}) copy-start(s32[16]{0:T(128)} %param.19) | copy-start | bytes 196
  7.2 51.2 %copy-start.69 = (s32[2]{0:T(128)S(1)}, s32[2]{0:T(128)}, u32[]{:S(2)}) copy-start(s32[2]{0:T(128)} %param.20) | copy-start | bytes 28
  7.2 65.6 %all-gather.16.cloned.1.call-start = ((), (), s32[]{:S(2)}) async-start(), calls=%async_computation.11 | async-start | bytes 1572864 | tf_op jit(solution)/shard_map/all_gather | solution.py:85
  8.4 42.3 %copy-start.53 = (f32[128]{0:T(128)}, f32[128]{0:T(128)S(1)}, u32[]{:S(2)}) copy-start(f32[128]{0:T(128)S(1)} %broadcast_multiply_fusion.10) | copy-start | bytes 1540
  9.8 41.0 %copy-start.60 = (f32[128]{0:T(128)}, f32[128]{0:T(128)S(1)}, u32[]{:S(2)}) copy-start(f32[128]{0:T(128)S(1)} %add_rsqrt_fusion.2) | copy-start | bytes 1540
  33.1 17.7 copy-start.43
  53.1 72.4 %all-gather.24.cloned.1.call-start = ((), (), s32[]{:S(2)}) async-start(), calls=%async_computation.15 | async-start | bytes 4456448 | tf_op jit(solution)/shard_map/all_gather | solution.py:123
  53.8 122.7 %all-gather.22.cloned.1.call-start = ((), (), s32[]{:S(2)}) async-start(), calls=%async_computation.14 | async-start | bytes 4456448 | tf_op jit(solution)/shard_map/all_gather | solution.py:122
  54.5 196.9 %all-gather.20.cloned.1.call-start = ((), (), s32[]{:S(2)}) async-start(), calls=%async_computation.13 | async-start | bytes 8912896 | tf_op jit(solution)/shard_map/all_gather | solution.py:124
  55.1 271.2 %all-gather.18.cloned.1.call-start = ((), (), s32[]{:S(2)}) async-start(), calls=%async_computation.12 | async-start | bytes 8912896 | tf_op jit(solution)/shard_map/all_gather | solution.py:125
  55.7 384.0 %all-reduce.10.cloned.1.call-start = ((), (), s32[]{:S(2)}) async-start(), calls=%async_computation.16 | async-start | bytes 8388608 | tf_op jit(solution)/shard_map/psum | solution.py:204
  61.6 378.1 %copy-start.57 = (f32[2]{0:T(128)}, f32[2]{0:T(128)S(1)}, u32[]{:S(2)}) copy-start(f32[2]{0:T(128)S(1)} %compare_convert_fusion) | copy-start | bytes 28
  62.3 201.7 %copy-start.66 = (f32[4]{0:T(128)}, f32[4]{0:T(128)S(1)}, u32[]{:S(2)}) copy-start(f32[4]{0:T(128)S(1)} %subtract_log_fusion) | copy-start | bytes 52
  62.4 194.7 %copy-start.46 = (f32[256,4]{0,1:T(4,128)}, f32[256,4]{0,1:T(4,128)S(1)}, u32[]{:S(2)}) copy-start(f32[256,4]{0,1:T(4,128)S(1)} %get-tuple-element.64) | copy-start | bytes 12292
  62.4 380.3 %copy-start.48 = (f32[256,4]{0,1:T(4,128)}, f32[256,4]{0,1:T(4,128)S(1)}, u32[]{:S(2)}) copy-start(f32[256,4]{0,1:T(4,128)S(1)} %get-tuple-element.65) | copy-start | bytes 12292
  129.2 47.4 %copy-start = (bf16[256,2048]{1,0:T(8,128)(2,1)S(1)}, bf16[256,2048]{1,0:T(8,128)(2,1)}, u32[]{:S(2)}) copy-start(bf16[256,2048]{1,0:T(8,128)(2,1)} %all-gather.16.cloned.1.call-done) | copy-start | bytes 3145732
  185.0 79.1 %copy-start.27 = (bf16[256,4,128]{2,0,1:T(8,128)(2,1)}, bf16[256,4,128]{2,0,1:T(8,128)(2,1)S(1)}, u32[]{:S(2)}) copy-start(bf16[256,4,128]{2,0,1:T(8,128)(2,1)S(1)} %get-tuple-element.51) | copy-start | bytes 786436
  257.1 80.0 %copy-start.5 = (bf16[256,2048]{1,0:T(8,128)(2,1)}, bf16[256,2048]{1,0:T(8,128)(2,1)S(1)}, u32[]{:S(2)}) copy-start(bf16[256,2048]{1,0:T(8,128)(2,1)S(1)} %convolution_convert_fusion) | copy-start | bytes 3145732
  261.1 254.1 %all-gather.26.cloned.1.call-start = ((), (), s32[]{:S(2)}) async-start(), calls=%async_computation.17 | async-start | bytes 8912896 | tf_op jit(solution)/shard_map/all_gather | solution.py:126
  261.9 298.4 %reduce-scatter.12.cloned.1.call-start = ((), (), s32[]{:S(2)}) async-start(), calls=%async_computation.18 | async-start | bytes 3145728 | tf_op jit(solution)/shard_map/reduce_scatter | solution.py:89
  262.7 2.6 copy-start.42
  264.1 178.7 %copy-start.13 = (bf16[256,4,256]{2,0,1:T(8,128)(2,1)}, bf16[256,4,256]{2,0,1:T(8,128)(2,1)S(1)}, u32[]{:S(2)}) copy-start(bf16[256,4,256]{2,0,1:T(8,128)(2,1)S(1)} %fusion.41) | copy-start | bytes 1572868
  334.1 3.0 copy-start.30
  439.7 3.0 copy-start.10
  445.8 76.6 %copy-start.17 = (bf16[256,4,512]{0,2,1:T(8,128)(2,1)}, bf16[256,4,512]{0,2,1:T(8,128)(2,1)S(1)}, u32[]{:S(2)}) copy-start(bf16[256,4,512]{0,2,1:T(8,128)(2,1)S(1)} %multiply_convert_fusion.3) | copy-start | bytes 3145732
  522.4 19.8 copy-start.65
  522.4 107.2 %all-gather.30.cloned.1.call-start = ((), (), s32[]{:S(2)}) async-start(), calls=%async_computation.20 | async-start | bytes 8912896 | tf_op jit(solution)/shard_map/all_gather | solution.py:131
  523.2 128.3 %all-gather.28.cloned.1.call-start = ((), (), s32[]{:S(2)}) async-start(), calls=%async_computation.19 | async-start | bytes 1572864 | tf_op jit(solution)/shard_map/all_gather | solution.py:85
  563.7 164.2 %all-gather.32.cloned.1.call-start = ((), (), s32[]{:S(2)}) async-start(), calls=%async_computation.21 | async-start | bytes 8912896 | tf_op jit(solution)/shard_map/all_gather | solution.py:132
  564.5 201.6 %reduce-scatter.14.cloned.1.call-start = ((), (), s32[]{:S(2)}) async-start(), calls=%async_computation.22 | async-start | bytes 3145728 | tf_op jit(solution)/shard_map/reduce_scatter | solution.py:89
  735.4 98.8 %all-gather.34.cloned.1.call-start = ((), (), s32[]{:S(2)}) async-start(), calls=%async_computation.23 | async-start | bytes 1572864 | tf_op jit(solution)/shard_map/all_gather | solution.py:85
  811.8 70.2 %reduce-scatter.16.cloned.1.call-start = ((), (), s32[]{:S(2)}) async-start(), calls=%async_computation.24 | async-start | bytes 3145728 | tf_op jit(solution)/shard_map/reduce_scatter | solution.py:89
  850.0 59.0 %all-gather.36.cloned.1.call-start = ((), (), s32[]{:S(2)}) async-start(), calls=%async_computation.25 | async-start | bytes 1572864 | tf_op jit(solution)/shard_map/all_gather | solution.py:85
  882.0 2.4 copy-start.59
  882.0 2.4 copy-start.63
  887.6 147.5 %all-reduce.12.cloned.1.call-start = ((), (), s32[]{:S(2)}) async-start(), calls=%async_computation.26 | async-start | bytes 8388608 | tf_op jit(solution)/shard_map/psum | solution.py:282
  909.0 7.2 copy-start.3
  923.8 198.8 %reduce-scatter.18.cloned.1.call-start = ((), (), s32[]{:S(2)}) async-start(), calls=%async_computation.27 | async-start | bytes 3145728 | tf_op jit(solution)/shard_map/reduce_scatter | solution.py:89
  923.9 3.5 copy-start.6
  923.9 3.5 copy-start.67
  927.4 3.0 copy-start.8
  931.4 3.1 copy-start.32
  936.7 101.4 %copy-start.12 = (f32[4,512,256]{2,1,0:T(8,128)S(1)}, f32[4,512,256]{2,1,0:T(8,128)}, u32[]{:S(2)}) copy-start(f32[4,512,256]{2,1,0:T(8,128)} %fusion.76) | copy-start | bytes 6291460
  936.7 101.4 %copy-start.47 = (f32[256,4]{0,1:T(4,128)S(1)}, f32[256,4]{0,1:T(4,128)}, u32[]{:S(2)}) copy-start(f32[256,4]{0,1:T(4,128)} %copy-done.46) | copy-start | bytes 12292
  1035.1 3.1 copy-start.29
  1041.9 3.7 copy-start.22
  1045.6 7.4 slice-start
  1047.0 6.0 copy-start.19
  1047.0 6.0 slice-start.1
  1056.9 139.8 %reduce-scatter.22.cloned.1.call-start = ((), (), s32[]{:S(2)}) async-start(), calls=%async_computation.29 | async-start | bytes 8912896 | tf_op jit(solution)/shard_map/reduce_scatter | solution.py:321
  1063.0 241.6 %reduce-scatter.20.cloned.1.call-start = ((), (), s32[]{:S(2)}) async-start(), calls=%async_computation.28 | async-start | bytes 8912896 | tf_op jit(solution)/shard_map/reduce_scatter | solution.py:320
  1067.7 418.4 %reduce-scatter.30.cloned.1.call-start = ((), (), s32[]{:S(2)}) async-start(), calls=%async_computation.33 | async-start | bytes 17825792 | tf_op jit(solution)/shard_map/reduce_scatter | solution.py:248
  1078.3 589.0 %reduce-scatter.32.cloned.1.call-start = ((), (), s32[]{:S(2)}) async-start(), calls=%async_computation.34 | async-start | bytes 17825792 | tf_op jit(solution)/shard_map/reduce_scatter | solution.py:249
  1088.9 759.5 %reduce-scatter.28.cloned.1.call-start = ((), (), s32[]{:S(2)}) async-start(), calls=%async_computation.32 | async-start | bytes 17825792 | tf_op jit(solution)/shard_map/reduce_scatter | solution.py:324
  1099.9 929.6 %reduce-scatter.26.cloned.1.call-start = ((), (), s32[]{:S(2)}) async-start(), calls=%async_computation.31 | async-start | bytes 17825792 | tf_op jit(solution)/shard_map/reduce_scatter | solution.py:323
  1110.0 1100.5 %reduce-scatter.24.cloned.1.call-start = ((), (), s32[]{:S(2)}) async-start(), calls=%async_computation.30 | async-start | bytes 17825792 | tf_op jit(solution)/shard_map/reduce_scatter | solution.py:322
  1119.4 3.2 copy-start.4
  1119.4 3.2 copy-start.44
  1119.4 3.2 copy-start.54
  1119.4 3.2 copy-start.61
  1119.4 5.0 copy-start.51
  1119.4 5.0 copy-start.52
  1119.5 73.6 %copy-start.23 = (f32[128,2048]{1,0:T(8,128)S(1)}, f32[128,2048]{1,0:T(8,128)}, u32[]{:S(2)}) copy-start(f32[128,2048]{1,0:T(8,128)} %get-tuple-element.36) | copy-start | bytes 3145732
  1122.7 70.4 %copy-start.21 = (f32[128,2048]{1,0:T(8,128)S(1)}, f32[128,2048]{1,0:T(8,128)}, u32[]{:S(2)}) copy-start(f32[128,2048]{1,0:T(8,128)} %reduce-scatter.18.cloned.1.call-done) | copy-start | bytes 3145732
  (33 other events, 44.4 us)
Sparse Core Ops, SparseCore 0:
  53.2 19.6 all-gather.15
  75.0 50.3 all-gather.23
  127.6 48.8 all-gather.21
  178.5 72.8 all-gather.19
  253.4 72.8 all-gather.17
  329.9 109.7 all-reduce.9
  441.8 73.4 all-gather.25
  522.5 30.4 reduce-scatter.11
  555.2 74.3 all-gather.29
  631.5 19.8 all-gather.27
  653.6 74.2 all-gather.31
  735.5 30.4 reduce-scatter.13
  812.0 22.1 all-gather.33
  850.1 31.8 reduce-scatter.15
  887.7 21.2 all-gather.35
  924.0 111.1 all-reduce.11
  1057.1 31.0 reduce-scatter.17
  1092.6 104.1 reduce-scatter.21
  1201.4 103.1 reduce-scatter.19
  1309.1 176.9 reduce-scatter.29
  1490.8 176.4 reduce-scatter.31
  1671.9 176.3 reduce-scatter.27
  1853.1 176.3 reduce-scatter.25
  2034.0 176.3 reduce-scatter.23
where the time goes:
time: 2230 us; the launch traced here: 2220 us
  waiting for transfers between devices  1780 us (80%)
  blocking collectives  185 us (8%)
  matrix products  155 us (7%)
  other arithmetic  51.2 us (2%)
  local copies, waits for them, and re-layouts  23 us (1%)
    reduce_scatter x1, waiting for transfers between devices, on_device(): lax.psum_scatter(grad_wu, 'dp', scatter_dimension=0, tiled=True)  182 us
    reduce_scatter x1, waiting for transfers between devices, on_device(): lax.psum_scatter(grad_wd, 'dp', scatter_dimension=0, tiled=True)  181 us
    reduce_scatter x1, waiting for transfers between devices, on_device(): lax.psum_scatter(grad_wg, 'dp', scatter_dimension=0, tiled=True)  181 us
    reduce_scatter x1, waiting for transfers between devices, on_device(): lax.psum_scatter(grad_wo, 'dp', scatter_dimension=0, tiled=True)  181 us
    reduce_scatter x1, waiting for transfers between devices, on_device(): lax.psum_scatter(grad_wv, 'dp', scatter_dimension=0, tiled=True)  181 us
    reduce_scatter x1, waiting for transfers between devices, on_device(): lax.psum_scatter(grad_wq, 'dp', scatter_dimension=0, tiled=True)  108 us
    psum x1, waiting for transfers between devices, on_device(): summed = lax.psum(slots, 'dp')  101 us
    psum x1, waiting for transfers between devices, on_device(): grad_summed = lax.psum(grad_slots, 'dp')  98.4 us
  transfers between devices with their start and end apart: 24, of which 22 were waited for; matrix products, arithmetic and copies ran while one was open for 6% of the time, Pallas kernels for 0%

commit v1 on v0

--- a/solution.py
+++ b/solution.py
@@ -279,7 +279,7 @@
         precision=lax.Precision.HIGHEST,
     )
     grad_slots = group_onehot[:, None, None, None] * state_grad_own[None]
-    grad_summed = lax.psum(grad_slots, "dp")
+    grad_summed = jnp.sum(lax.all_gather(grad_slots, "dp"), axis=0)
     state_gradient = (
         prompt_flag * jnp.sum(grad_summed * group_onehot[:, None, None, None], axis=0)
     ).astype(jnp.bfloat16)

time: 2230 us -> 2470 us (1.11)
  waiting for transfers between devices: 1780 us -> 1990 us
    all_gather x0 -> x1, waiting for transfers between devices: none -> 314 us  [on_device(): grad_summed = jnp.sum(lax.all_gather(grad_slots, 'dp'), axis=0)]
    reduce_scatter x1, waiting for transfers between devices: 182 us -> 71.9 us  [on_device(): lax.psum_scatter(grad_wu, 'dp', scatter_dimension=0, tiled=True)]
    reduce_scatter x1, waiting for transfers between devices: 2.26 us -> 107 us  [on_device(): lax.psum_scatter(grad_wk, 'dp', scatter_dimension=0, tiled=True)]
    psum x1 -> x0, waiting for transfers between devices: 98.4 us -> none  [on_device(): grad_summed = lax.psum(grad_slots, 'dp')]
where the time goes in v1:
time: 2470 us; the launch traced here: 2460 us
  waiting for transfers between devices  1990 us (81%)
  blocking collectives  188 us (8%)
  matrix products  159 us (6%)
  other arithmetic  74 us (3%)
    all_gather x1, waiting for transfers between devices, on_device(): grad_summed = jnp.sum(lax.all_gather(grad_slots, 'dp'), axis=0)  314 us
    reduce_scatter x1, waiting for transfers between devices, on_device(): lax.psum_scatter(grad_wv, 'dp', scatter_dimension=0, tiled=True)  182 us
    reduce_scatter x1, waiting for transfers between devices, on_device(): lax.psum_scatter(grad_wd, 'dp', scatter_dimension=0, tiled=True)  181 us
    reduce_scatter x1, waiting for transfers between devices, on_device(): lax.psum_scatter(grad_wg, 'dp', scatter_dimension=0, tiled=True)  181 us
    reduce_scatter x1, waiting for transfers between devices, on_device(): lax.psum_scatter(grad_wo, 'dp', scatter_dimension=0, tiled=True)  181 us
    reduce_scatter x1, waiting for transfers between devices, on_device(): lax.psum_scatter(grad_wq, 'dp', scatter_dimension=0, tiled=True)  108 us
    reduce_scatter x1, waiting for transfers between devices, on_device(): lax.psum_scatter(grad_wk, 'dp', scatter_dimension=0, tiled=True)  107 us
    psum x1, waiting for transfers between devices, on_device(): summed = lax.psum(slots, 'dp')  101 us
  transfers between devices with their start and end apart: 24, of which 22 were waited for; matrix products, arithmetic and copies ran while one was open for 6% of the time, Pallas kernels for 0%

profile of v1, /device:TPU:0, one launch (start us, length us, event | category | flops | bytes accessed | tf_op | source)
XLA Modules:
  0.0 2458.4 jit_solution(11405579621670392804)
XLA Ops:
  9.8 23.3 all-gather
  33.1 17.6 all-gather.1
  50.8 2.2 fusion.28
  64.5 8.3 all-gather.17.cloned.1.call-done
  72.8 52.6 %all-gather.25.cloned.1.call-done = bf16[2048,1024]{1,0:T(8,128)(2,1)} async-done(((bf16[128,1024]{1,0:T(8,128)(2,1)}), bf16[2048,1024]{1,0:T(8,128)(2,1)}) %all-gather.25.cloned.1.call-update) | async-done | bytes 4194320 | tf_op jit(solution)/shard_map/all_gather | solution.py:123
  125.4 3.8 fusion.70
  129.7 46.8 %all-gather.23.cloned.1.call-done = bf16[2048,1024]{1,0:T(8,128)(2,1)} async-done(((bf16[128,1024]{1,0:T(8,128)(2,1)}), bf16[2048,1024]{1,0:T(8,128)(2,1)}) %all-gather.23.cloned.1.call-update) | async-done | bytes 4194320 | tf_op jit(solution)/shard_map/all_gather | solution.py:122
  176.5 4.4 fusion.69
  185.0 66.4 %all-gather.21.cloned.1.call-done = bf16[2048,2048]{1,0:T(8,128)(2,1)} async-done(((bf16[128,2048]{1,0:T(8,128)(2,1)}), bf16[2048,2048]{1,0:T(8,128)(2,1)}) %all-gather.21.cloned.1.call-update) | async-done | bytes 8388624 | tf_op jit(solution)/shard_map/all_gather | solution.py:124
  251.4 5.7 convolution_convert_fusion
  258.5 2.5 broadcast_multiply_fusion.1
  265.0 61.3 %all-gather.19.cloned.1.call-done = bf16[2048,2048]{1,0:T(8,128)(2,1)} async-done(((bf16[128,2048]{1,0:T(8,128)(2,1)}), bf16[2048,2048]{1,0:T(8,128)(2,1)}) %all-gather.19.cloned.1.call-update) | async-done | bytes 8388624 | tf_op jit(solution)/shard_map/all_gather | solution.py:125
  326.3 7.9 fusion.12
  334.2 3.0 copy.151
  337.2 2.0 fusion.36
  339.1 100.5 %all-reduce.9.cloned.1.call-done = f32[2,4,256,512]{3,2,1,0:T(8,128)} async-done(((f32[2,4,256,512]{3,2,1,0:T(8,128)}), f32[2,4,256,512]{3,2,1,0:T(8,128)}) %all-reduce.9.cloned.1.call-update) | async-done | bytes 4194320 | tf_op jit(solution)/shard_map/psum | solution.py:204
  439.7 3.0 multiply_reduce_fusion.1
  445.8 69.5 %all-gather.27.cloned.1.call-done = bf16[2048,2048]{1,0:T(8,128)(2,1)} async-done(((bf16[128,2048]{1,0:T(8,128)(2,1)}), bf16[2048,2048]{1,0:T(8,128)(2,1)}) %all-gather.27.cloned.1.call-update) | async-done | bytes 8388624 | tf_op jit(solution)/shard_map/all_gather | solution.py:126
  515.3 7.2 fusion.71
  523.3 19.0 all-gather.2
  542.3 17.4 all-gather.3
  565.1 64.5 %all-gather.31.cloned.1.call-done = bf16[2048,2048]{1,0:T(8,128)(2,1)} async-done(((bf16[128,2048]{1,0:T(8,128)(2,1)}), bf16[2048,2048]{1,0:T(8,128)(2,1)}) %all-gather.31.cloned.1.call-update) | async-done | bytes 8388624 | tf_op jit(solution)/shard_map/all_gather | solution.py:131
  629.7 21.9 all-gather.29.cloned.1.call-done
  651.5 10.6 multiply_convert_fusion.2
  662.2 65.9 %all-gather.33.cloned.1.call-done = bf16[2048,2048]{1,0:T(8,128)(2,1)} async-done(((bf16[128,2048]{1,0:T(8,128)(2,1)}), bf16[2048,2048]{1,0:T(8,128)(2,1)}) %all-gather.33.cloned.1.call-update) | async-done | bytes 8388624 | tf_op jit(solution)/shard_map/all_gather | solution.py:132
  728.0 7.5 fusion.72
  735.6 2.4 fusion.63
  738.0 28.2 %reduce-scatter.14.cloned.1.call-done = f32[128,2048]{1,0:T(8,128)} async-done(((f32[256,2048]{1,0:T(8,128)}), f32[128,2048]{1,0:T(8,128)}) %reduce-scatter.14.cloned.1.call-update) | async-done | bytes 1048592 | tf_op jit(solution)/shard_map/reduce_scatter | solution.py:89
  766.2 3.2 fusion.35
  769.4 39.5 %all-reduce.4 = (f32[]{:T(128)}, f32[]{:T(128)}) all-reduce(f32[]{:T(128)} %get-tuple-element.39, f32[]{:T(128)} %get-tuple-element.37), channel_id=1, replica_groups=mesh['dp'=16,'mp'=2] {'dp','mp'}, use_global_device_ids=true, to_apply=%region_14.15 | all-reduce | flops 2 | bytes 16 | tf_op jit(solution)/shard_map/psum | solution.py:230
  809.6 2.3 fusion.47
  812.1 22.3 all-gather.35.cloned.1.call-done
  834.4 8.0 add_convert_fusion
  843.3 7.2 fusion.73
  850.7 31.8 %reduce-scatter.16.cloned.1.call-done = f32[128,2048]{1,0:T(8,128)} async-done(((f32[256,2048]{1,0:T(8,128)}), f32[128,2048]{1,0:T(8,128)}) %reduce-scatter.16.cloned.1.call-update) | async-done | bytes 1048592 | tf_op jit(solution)/shard_map/reduce_scatter | solution.py:89
  882.6 2.4 multiply_reduce_fusion.4
  885.0 3.1 fusion.62
  888.2 21.4 all-gather.37.cloned.1.call-done
  909.5 7.2 fusion.74
  919.7 2.0 fusion.42
  921.7 2.7 broadcast_multiply_fusion
  924.5 3.0 copy.150
  937.0 313.7 %all-gather.39.cloned.1.call-done = f32[16,2,4,256,512]{4,3,2,1,0:T(8,128)} async-done(((f32[1,2,4,256,512]{4,3,2,1,0:T(8,128)}), f32[16,2,4,256,512]{4,3,2,1,0:T(8,128)}) %all-gather.39.cloned.1.call-update) | async-done | bytes 67108880 | tf_op jit(solution)/shard_map/all_gather | solution.py:282
  1250.7 23.4 reduce_sum.221
  1274.1 3.2 multiply_reduce_fusion
  1281.1 3.6 fusion.75
  1286.1 6.0 convolution_add_fusion.2
  1292.1 3.7 convolution_add_fusion.1
  1297.0 9.8 fusion.82
  1308.1 9.4 fusion.83
  1318.7 9.4 fusion.81
  1329.3 8.3 fusion.80
  1337.7 5.7 fusion.78
  1343.5 5.9 fusion.77
  1350.8 10.3 fusion.79
  1366.1 65.2 %all-reduce.5 = (f32[2048]{0:T(1024)S(1)}, f32[2048]{0:T(1024)S(1)}, f32[2048]{0:T(1024)S(1)}, f32[2048]{0:T(1024)S(1)}) all-reduce(f32[2048]{0:T(1024)S(1)} %get-tuple-element.18, f32[2048]{0:T(1024)S(1)} %get-tuple-element.23, f32[2048]{0:T(1024)S(1)} %copy-done.50, ...), channel_id=6, replica_groups=mesh['dp'=16,'mp'=2] {'dp'}, use_global_device_ids=true, to_apply=%region_28.29.clone | all-reduce | flops 8192 | bytes 65536
  1431.6 5.4 all-reduce.6
  1438.5 71.9 %reduce-scatter.30.cloned.1.call-done = f32[128,2048]{1,0:T(8,128)} async-done(((f32[2048,2048]{1,0:T(8,128)}), f32[128,2048]{1,0:T(8,128)}) %reduce-scatter.30.cloned.1.call-update) | async-done | bytes 1048592 | tf_op jit(solution)/shard_map/reduce_scatter | solution.py:248
  1510.4 181.2 %reduce-scatter.32.cloned.1.call-done = f32[128,2048]{1,0:T(8,128)} async-done(((f32[2048,2048]{1,0:T(8,128)}), f32[128,2048]{1,0:T(8,128)}) %reduce-scatter.32.cloned.1.call-update) | async-done | bytes 1048592 | tf_op jit(solution)/shard_map/reduce_scatter | solution.py:249
  1691.6 181.0 %reduce-scatter.28.cloned.1.call-done = f32[128,2048]{1,0:T(8,128)} async-done(((f32[2048,2048]{1,0:T(8,128)}), f32[128,2048]{1,0:T(8,128)}) %reduce-scatter.28.cloned.1.call-update) | async-done | bytes 1048592 | tf_op jit(solution)/shard_map/reduce_scatter | solution.py:324
  1872.6 181.1 %reduce-scatter.26.cloned.1.call-done = f32[128,2048]{1,0:T(8,128)} async-done(((f32[2048,2048]{1,0:T(8,128)}), f32[128,2048]{1,0:T(8,128)}) %reduce-scatter.26.cloned.1.call-update) | async-done | bytes 1048592 | tf_op jit(solution)/shard_map/reduce_scatter | solution.py:323
  2053.7 107.2 %reduce-scatter.22.cloned.1.call-done = f32[128,1024]{1,0:T(8,128)} async-done(((f32[2048,1024]{1,0:T(8,128)}), f32[128,1024]{1,0:T(8,128)}) %reduce-scatter.22.cloned.1.call-update) | async-done | bytes 524304 | tf_op jit(solution)/shard_map/reduce_scatter | solution.py:321
  2160.9 107.8 %reduce-scatter.20.cloned.1.call-done = f32[128,1024]{1,0:T(8,128)} async-done(((f32[2048,1024]{1,0:T(8,128)}), f32[128,1024]{1,0:T(8,128)}) %reduce-scatter.20.cloned.1.call-update) | async-done | bytes 524304 | tf_op jit(solution)/shard_map/reduce_scatter | solution.py:320
  2268.7 181.6 %reduce-scatter.24.cloned.1.call-done = f32[128,2048]{1,0:T(8,128)} async-done(((f32[2048,2048]{1,0:T(8,128)}), f32[128,2048]{1,0:T(8,128)}) %reduce-scatter.24.cloned.1.call-update) | async-done | bytes 1048592 | tf_op jit(solution)/shard_map/reduce_scatter | solution.py:322
  (266 shorter events, 60.8 us)
Async XLA Ops:
  7.2 48.6 %copy-start.67 = (s32[16]{0:T(128)S(1)}, s32[16]{0:T(128)}, u32[]{:S(2)}) copy-start(s32[16]{0:T(128)} %param.19) | copy-start | bytes 196
  7.2 51.2 %copy-start.68 = (s32[2]{0:T(128)S(1)}, s32[2]{0:T(128)}, u32[]{:S(2)}) copy-start(s32[2]{0:T(128)} %param.20) | copy-start | bytes 28
  7.2 65.6 %all-gather.17.cloned.1.call-start = ((), (), s32[]{:S(2)}) async-start(), calls=%async_computation.11 | async-start | bytes 1572864 | tf_op jit(solution)/shard_map/all_gather | solution.py:85
  8.4 42.3 %copy-start.52 = (f32[128]{0:T(128)}, f32[128]{0:T(128)S(1)}, u32[]{:S(2)}) copy-start(f32[128]{0:T(128)S(1)} %broadcast_multiply_fusion.10) | copy-start | bytes 1540
  9.8 41.0 %copy-start.59 = (f32[128]{0:T(128)}, f32[128]{0:T(128)S(1)}, u32[]{:S(2)}) copy-start(f32[128]{0:T(128)S(1)} %add_rsqrt_fusion.2) | copy-start | bytes 1540
  33.1 17.7 copy-start.42
  53.1 72.4 %all-gather.25.cloned.1.call-start = ((), (), s32[]{:S(2)}) async-start(), calls=%async_computation.15 | async-start | bytes 4456448 | tf_op jit(solution)/shard_map/all_gather | solution.py:123
  53.8 122.7 %all-gather.23.cloned.1.call-start = ((), (), s32[]{:S(2)}) async-start(), calls=%async_computation.14 | async-start | bytes 4456448 | tf_op jit(solution)/shard_map/all_gather | solution.py:122
  54.5 196.9 %all-gather.21.cloned.1.call-start = ((), (), s32[]{:S(2)}) async-start(), calls=%async_computation.13 | async-start | bytes 8912896 | tf_op jit(solution)/shard_map/all_gather | solution.py:124
  55.1 271.2 %all-gather.19.cloned.1.call-start = ((), (), s32[]{:S(2)}) async-start(), calls=%async_computation.12 | async-start | bytes 8912896 | tf_op jit(solution)/shard_map/all_gather | solution.py:125
  55.7 384.0 %all-reduce.9.cloned.1.call-start = ((), (), s32[]{:S(2)}) async-start(), calls=%async_computation.16 | async-start | bytes 8388608 | tf_op jit(solution)/shard_map/psum | solution.py:204
  61.6 378.1 %copy-start.56 = (f32[2]{0:T(128)}, f32[2]{0:T(128)S(1)}, u32[]{:S(2)}) copy-start(f32[2]{0:T(128)S(1)} %compare_convert_fusion) | copy-start | bytes 28
  62.3 201.5 %copy-start.65 = (f32[4]{0:T(128)}, f32[4]{0:T(128)S(1)}, u32[]{:S(2)}) copy-start(f32[4]{0:T(128)S(1)} %subtract_log_fusion) | copy-start | bytes 52
  62.4 194.7 %copy-start.45 = (f32[256,4]{0,1:T(4,128)}, f32[256,4]{0,1:T(4,128)S(1)}, u32[]{:S(2)}) copy-start(f32[256,4]{0,1:T(4,128)S(1)} %get-tuple-element.64) | copy-start | bytes 12292
  62.4 380.3 %copy-start.47 = (f32[256,4]{0,1:T(4,128)}, f32[256,4]{0,1:T(4,128)S(1)}, u32[]{:S(2)}) copy-start(f32[256,4]{0,1:T(4,128)S(1)} %get-tuple-element.65) | copy-start | bytes 12292
  129.2 47.4 %copy-start = (bf16[256,2048]{1,0:T(8,128)(2,1)S(1)}, bf16[256,2048]{1,0:T(8,128)(2,1)}, u32[]{:S(2)}) copy-start(bf16[256,2048]{1,0:T(8,128)(2,1)} %all-gather.17.cloned.1.call-done) | copy-start | bytes 3145732
  185.0 78.8 %copy-start.26 = (bf16[256,4,128]{2,0,1:T(8,128)(2,1)}, bf16[256,4,128]{2,0,1:T(8,128)(2,1)S(1)}, u32[]{:S(2)}) copy-start(bf16[256,4,128]{2,0,1:T(8,128)(2,1)S(1)} %get-tuple-element.51) | copy-start | bytes 786436
  257.1 80.1 %copy-start.5 = (bf16[256,2048]{1,0:T(8,128)(2,1)}, bf16[256,2048]{1,0:T(8,128)(2,1)S(1)}, u32[]{:S(2)}) copy-start(bf16[256,2048]{1,0:T(8,128)(2,1)S(1)} %convolution_convert_fusion) | copy-start | bytes 3145732
  261.1 254.2 %all-gather.27.cloned.1.call-start = ((), (), s32[]{:S(2)}) async-start(), calls=%async_computation.17 | async-start | bytes 8912896 | tf_op jit(solution)/shard_map/all_gather | solution.py:126
  261.8 298.6 %reduce-scatter.12.cloned.1.call-start = ((), (), s32[]{:S(2)}) async-start(), calls=%async_computation.18 | async-start | bytes 3145728 | tf_op jit(solution)/shard_map/reduce_scatter | solution.py:89
  262.4 2.6 copy-start.41
  263.8 178.9 %copy-start.13 = (bf16[256,4,256]{2,0,1:T(8,128)(2,1)}, bf16[256,4,256]{2,0,1:T(8,128)(2,1)S(1)}, u32[]{:S(2)}) copy-start(bf16[256,4,256]{2,0,1:T(8,128)(2,1)S(1)} %fusion.41) | copy-start | bytes 1572868
  334.2 3.0 copy-start.29
  439.7 3.0 copy-start.10
  445.8 76.7 %copy-start.17 = (bf16[256,4,512]{0,2,1:T(8,128)(2,1)}, bf16[256,4,512]{0,2,1:T(8,128)(2,1)S(1)}, u32[]{:S(2)}) copy-start(bf16[256,4,512]{0,2,1:T(8,128)(2,1)S(1)} %multiply_convert_fusion.3) | copy-start | bytes 3145732
  522.5 19.8 copy-start.64
  522.5 107.2 %all-gather.31.cloned.1.call-start = ((), (), s32[]{:S(2)}) async-start(), calls=%async_computation.20 | async-start | bytes 8912896 | tf_op jit(solution)/shard_map/all_gather | solution.py:131
  523.3 128.3 %all-gather.29.cloned.1.call-start = ((), (), s32[]{:S(2)}) async-start(), calls=%async_computation.19 | async-start | bytes 1572864 | tf_op jit(solution)/shard_map/all_gather | solution.py:85
  563.8 164.2 %all-gather.33.cloned.1.call-start = ((), (), s32[]{:S(2)}) async-start(), calls=%async_computation.21 | async-start | bytes 8912896 | tf_op jit(solution)/shard_map/all_gather | solution.py:132
  564.6 201.6 %reduce-scatter.14.cloned.1.call-start = ((), (), s32[]{:S(2)}) async-start(), calls=%async_computation.22 | async-start | bytes 3145728 | tf_op jit(solution)/shard_map/reduce_scatter | solution.py:89
  735.6 98.8 %all-gather.35.cloned.1.call-start = ((), (), s32[]{:S(2)}) async-start(), calls=%async_computation.23 | async-start | bytes 1572864 | tf_op jit(solution)/shard_map/all_gather | solution.py:85
  812.0 70.6 %reduce-scatter.16.cloned.1.call-start = ((), (), s32[]{:S(2)}) async-start(), calls=%async_computation.24 | async-start | bytes 3145728 | tf_op jit(solution)/shard_map/reduce_scatter | solution.py:89
  850.5 59.0 %all-gather.37.cloned.1.call-start = ((), (), s32[]{:S(2)}) async-start(), calls=%async_computation.25 | async-start | bytes 1572864 | tf_op jit(solution)/shard_map/all_gather | solution.py:85
  882.6 2.4 copy-start.58
  882.6 2.4 copy-start.62
  888.1 362.6 %all-gather.39.cloned.1.call-start = ((), (), s32[]{:S(2)}) async-start(), calls=%async_computation.26 | async-start | bytes 71303168 | tf_op jit(solution)/shard_map/all_gather | solution.py:282
  909.5 7.2 copy-start.3
  924.4 439.8 %reduce-scatter.18.cloned.1.call-start = ((), (), s32[]{:S(2)}) async-start(), calls=%async_computation.27 | async-start | bytes 3145728 | tf_op jit(solution)/shard_map/reduce_scatter | solution.py:89
  924.5 3.0 copy-start.6
  924.5 3.0 copy-start.66
  927.5 3.0 copy-start.8
  931.6 3.1 copy-start.31
  932.8 3.0 copy-start.11
  1274.1 3.2 copy-start.12
  1274.1 3.2 copy-start.28
  1274.1 3.2 copy-start.46
  1281.1 3.7 copy-start.21
  1284.7 7.3 slice-start
  1286.1 6.0 slice-start.1
  1295.8 214.6 %reduce-scatter.30.cloned.1.call-start = ((), (), s32[]{:S(2)}) async-start(), calls=%async_computation.33 | async-start | bytes 17825792 | tf_op jit(solution)/shard_map/reduce_scatter | solution.py:248
  1306.9 384.7 %reduce-scatter.32.cloned.1.call-start = ((), (), s32[]{:S(2)}) async-start(), calls=%async_computation.34 | async-start | bytes 17825792 | tf_op jit(solution)/shard_map/reduce_scatter | solution.py:249
  1317.5 555.1 %reduce-scatter.28.cloned.1.call-start = ((), (), s32[]{:S(2)}) async-start(), calls=%async_computation.32 | async-start | bytes 17825792 | tf_op jit(solution)/shard_map/reduce_scatter | solution.py:324
  1328.1 725.6 %reduce-scatter.26.cloned.1.call-start = ((), (), s32[]{:S(2)}) async-start(), calls=%async_computation.31 | async-start | bytes 17825792 | tf_op jit(solution)/shard_map/reduce_scatter | solution.py:323
  1337.6 823.3 %reduce-scatter.22.cloned.1.call-start = ((), (), s32[]{:S(2)}) async-start(), calls=%async_computation.29 | async-start | bytes 8912896 | tf_op jit(solution)/shard_map/reduce_scatter | solution.py:321
  1343.4 925.3 %reduce-scatter.20.cloned.1.call-start = ((), (), s32[]{:S(2)}) async-start(), calls=%async_computation.28 | async-start | bytes 8912896 | tf_op jit(solution)/shard_map/reduce_scatter | solution.py:320
  1349.3 1100.9 %reduce-scatter.24.cloned.1.call-start = ((), (), s32[]{:S(2)}) async-start(), calls=%async_computation.30 | async-start | bytes 17825792 | tf_op jit(solution)/shard_map/reduce_scatter | solution.py:322
  1361.0 3.2 copy-start.4
  1361.0 3.2 copy-start.43
  1361.0 3.2 copy-start.53
  1361.0 3.2 copy-start.60
  1361.1 5.0 copy-start.50
  1361.1 5.0 copy-start.51
  1361.1 76.0 %copy-start.22 = (f32[128,2048]{1,0:T(8,128)S(1)}, f32[128,2048]{1,0:T(8,128)}, u32[]{:S(2)}) copy-start(f32[128,2048]{1,0:T(8,128)} %get-tuple-element.36) | copy-start | bytes 3145732
  1364.3 72.8 %copy-start.20 = (f32[128,2048]{1,0:T(8,128)S(1)}, f32[128,2048]{1,0:T(8,128)}, u32[]{:S(2)}) copy-start(f32[128,2048]{1,0:T(8,128)} %reduce-scatter.18.cloned.1.call-done) | copy-start | bytes 3145732
  (32 other events, 42.4 us)
Sparse Core Ops, SparseCore 0:
  53.2 19.6 all-gather.16
  75.0 50.3 all-gather.24
  127.6 48.8 all-gather.22
  178.5 72.8 all-gather.20
  253.4 72.8 all-gather.18
  329.9 109.7 all-reduce.8
  441.8 73.4 all-gather.26
  522.6 30.4 reduce-scatter.11
  555.3 74.3 all-gather.30
  631.6 19.8 all-gather.28
  653.7 74.2 all-gather.32
  735.7 30.4 reduce-scatter.13
  812.1 22.1 all-gather.34
  850.6 31.8 reduce-scatter.15
  888.2 21.2 all-gather.36
  924.5 326.0 all-gather.38
  1295.9 31.8 reduce-scatter.17
  1332.4 178.0 reduce-scatter.29
  1515.1 176.4 reduce-scatter.31
  1696.1 176.4 reduce-scatter.27
  1877.3 176.4 reduce-scatter.25
  2058.4 102.5 reduce-scatter.21
  2165.6 103.0 reduce-scatter.19
  2273.2 176.9 reduce-scatter.23
